TPU v7x, 128 devices: a whole 4x4x4 slice. The times are simulated.
128 devices in a mesh: col: 64 (over z, y, x_hi, core), seq: 2 (over x_lo).
Axes of the slice: x: 4 (x_hi: 2, x_lo: 2; x = x_hi * 2 + x_lo), y: 4, z: 4, core: 2. Of those that a mesh axis runs over, the one named last changes fastest.
Arguments:
- history_items: int32 [64, 1024], P(None, 'seq'), may hold values from 0 to 65535
- lengths: int32 [64], replicated, may hold values from 64 to 1024, as said below
- item_table: float32 [512, 65536], P('col'), may hold values from -4 to 4
- input_weight: bfloat16 [512, 2048], replicated, may hold values from -0.25 to 0.25
- output_weight: bfloat16 [512, 512], replicated, may hold values from -0.25 to 0.25
- output_cotangent: bfloat16 [64, 1024, 512], P('col', 'seq'), may hold values from -6 to 6
Outputs:
- layer_output: bfloat16 [64, 1024, 512], P('col', 'seq')
- table_gradient: float32 [512, 65536], P('col', 'seq')
Inputs may be any that keep to these rules, and one draw needn't show every extreme that they name: `lengths`: in every draw one history has exactly 1024 items.
All inputs are finite; a program needn't handle non-finite values.
Results may differ from a plain program's by a relative error of at most 0.0077.
Values may be sent and summed in bfloat16 or wider, within the bound.
No kernel may reach another device: no remote copies, remote signals or barrier semaphores. Data moves between devices by JAX's collectives and lax.ppermute only.
A program may use at most 128 MiB of HBM per device.

v0:
```python
import jax
import jax.numpy as jnp
from jax import lax
from jax.experimental import pallas as pl
from jax.experimental.pallas import tpu as pltpu
from jax.sharding import PartitionSpec as P

H = 8
DH = 64
LEN = 1024
D = 512
HID = H * DH
USERS = 64
FEAT = 8
HALF = 512
BLK = 128
NBLK = HALF // BLK
ROWS = 65536
PAIRS = H // 2
norm_epsilon = 1e-05
bf16 = jnp.bfloat16
f32 = jnp.float32

G_LO = 16
G_HI = ROWS // G_LO
G_STEP = 8
S_ROWS = ROWS // 2
S_LO = 32
S_HI = S_ROWS // S_LO
S_STEP = 16


def block_list(seq, lengths_ref, list_ref):
    def step(u, count):
        parity = (seq + u) & 1
        blocks = (lengths_ref[u] + (BLK - 1)) >> 7
        for i in range(NBLK):
            list_ref[count + i] = u * NBLK + i
        return count + ((blocks + 1 - parity) >> 1)

    return lax.fori_loop(0, USERS, step, 0)


def item_row(items_ref, seq, block):
    u = block >> 2
    i = block & 3
    parity = (seq + u) & 1
    return items_ref[i >> 1, 2 * (i & 1) + parity, pl.ds(u, 1), :]


def stage_items(seq, own_ref, other_ref, items_ref):
    for b in range(NBLK):
        items_ref[seq, b] = own_ref[:, b * BLK : (b + 1) * BLK]
        items_ref[1 - seq, b] = other_ref[:, b * BLK : (b + 1) * BLK]


def onehot(index, rows):
    n = index.shape[1]
    iota = lax.broadcasted_iota(jnp.int16, (rows, n), 0)
    wide = jnp.broadcast_to(index.astype(jnp.int16), (rows, n))
    return jnp.where(iota == wide, jnp.ones((), bf16), jnp.zeros((), bf16))


def rows_kernel(table_ref, rows_ref):
    step = 512
    for c in range(G_HI // step):
        parts = [
            table_ref[:, lo * G_HI + c * step : lo * G_HI + (c + 1) * step] for lo in range(G_LO)
        ]
        rows_ref[c * step : (c + 1) * step, :] = jnp.concatenate(parts, axis=0).T


def gather_kernel(
    seq_ref, lengths_ref, own_ref, other_ref, rows_ref, out_ref,
    items_ref, stage_ref, got_ref, list_ref, index_ref, sems,
):
    seq = seq_ref[0]
    stage_items(seq, own_ref, other_ref, items_ref)
    out_ref[...] = jnp.zeros_like(out_ref)
    count = block_list(seq, lengths_ref, list_ref)
    pairs = (count + 2 * G_STEP - 1) // (2 * G_STEP)

    def ids_of(g):
        last = count - 1
        return [list_ref[jnp.minimum(g * G_STEP + j, last)] for j in range(G_STEP)]

    def copy(slot):
        return pltpu.make_async_copy(stage_ref.at[slot], index_ref.at[slot], sems.at[slot])

    def fetch(g, slot):
        rows = jnp.concatenate([item_row(items_ref, seq, b) for b in ids_of(g)], axis=0)
        stage_ref[slot] = rows & (G_HI - 1)
        copy(slot).start()

    def move(slot):
        for j in range(G_STEP):
            for t in range(BLK):
                r = index_ref[slot, j, t]
                got_ref[slot, pl.ds(j * BLK + t, 1), :] = rows_ref[pl.ds(r, 1), :]

    def finish(g, slot):
        ids = ids_of(g)
        for j in range(G_STEP):
            u = ids[j] >> 2
            col = pl.multiple_of((ids[j] & 3) * BLK, BLK)
            lo = lax.shift_right_logical(item_row(items_ref, seq, ids[j]), 12)
            part = got_ref[slot, j * BLK : (j + 1) * BLK, :].T.reshape(G_LO, FEAT, BLK)
            mask = lax.broadcasted_iota(jnp.int32, (G_LO, FEAT, BLK), 0) == lo.reshape(1, 1, BLK)
            part = jnp.sum(jnp.where(mask, part, 0.0), axis=0).astype(bf16)
            out_ref[u, 0, :, pl.ds(col, BLK)] = part
            out_ref[u, 1, :, pl.ds(col, BLK)] = part

    got_ref[1] = jnp.zeros_like(got_ref[1])
    for slot in range(2):
        fetch(slot, slot)

    def step(p, carry):
        for slot in range(2):
            g = 2 * p + slot
            copy(slot).wait()
            move(slot)
            finish(jnp.maximum(g - 1, 0), 1 - slot)
            fetch(g + 2, slot)
        return carry

    lax.fori_loop(0, pairs, step, 0)
    finish(2 * pairs - 1, 1)
    for slot in range(2):
        copy(slot).wait()


def scatter_kernel(
    seq_ref, lengths_ref, half_ref, own_ref, other_ref, grad_ref, out_ref, items_ref, acc_ref, list_ref
):
    seq = seq_ref[0]
    base = half_ref[0] * S_ROWS
    stage_items(seq, own_ref, other_ref, items_ref)
    acc_ref[...] = jnp.zeros_like(acc_ref)
    count = block_list(seq, lengths_ref, list_ref)

    def step(g, carry):
        rows, grads = [], []
        for j in range(S_STEP):
            at = g * S_STEP + j
            b = list_ref[jnp.maximum(jnp.minimum(at, count - 1), 0)]
            row = item_row(items_ref, seq, b) - base
            rows.append(jnp.where(at < count, row, -1))
            u = b >> 2
            col = pl.multiple_of((b & 3) * BLK, BLK)
            grads.append(
                grad_ref[u, 0, :, pl.ds(col, BLK)].astype(f32)
                + grad_ref[u, 1, :, pl.ds(col, BLK)].astype(f32)
            )
        index = jnp.concatenate(rows, axis=1)
        grad = jnp.concatenate(grads, axis=1)
        n = S_STEP * BLK
        lo = lax.shift_right_arithmetic(index, 10)
        hi = index & (S_HI - 1)
        mask = lax.broadcasted_iota(jnp.int32, (S_LO, FEAT, n), 0) == lo.reshape(1, 1, n)
        spread = jnp.where(mask, jnp.broadcast_to(grad[None], (S_LO, FEAT, n)), 0.0)
        spread = spread.reshape(S_LO * FEAT, n).astype(bf16)
        acc_ref[...] += lax.dot_general(
            spread, onehot(hi, S_HI), (((1,), (1,)), ((), ())), preferred_element_type=f32
        )
        return carry

    lax.fori_loop(0, (count + S_STEP - 1) // S_STEP, step, 0)
    for lo in range(S_LO):
        out_ref[:, lo * S_HI : (lo + 1) * S_HI] = acc_ref[lo * FEAT : (lo + 1) * FEAT, :].astype(
            out_ref.dtype
        )


def dot_nt(a, b):
    return lax.dot_general(a, b, (((1,), (1,)), ((), ())), preferred_element_type=f32)


def dot_nn(a, b):
    return jnp.dot(a, b, preferred_element_type=f32)


def norm(z):
    m = jnp.mean(z, axis=-1, keepdims=True)
    c = z - m
    w = jnp.mean(c * c, axis=-1, keepdims=True)
    r = lax.rsqrt(w + norm_epsilon)
    return c * r, r


def norm_back(y, r, dy):
    a = jnp.mean(dy, axis=-1, keepdims=True)
    b = jnp.mean(dy * y, axis=-1, keepdims=True)
    return r * (dy - a - y * b)


def gate(h):
    t = jnp.tanh(h)
    a = 1.0 + t
    act = h * a
    return act, a + act * (1.0 - t)


def slope_of(a, p):
    return a + p.astype(f32) * (2.0 - a)


def layer_kernel(
    seq_ref, col_ref, lengths_ref, e_ref, w_hbm, wo_hbm, cot_hbm, out_ref, g_ref,
    w_ref, wo_ref, cot_ref, sems,
    x_ref, y_ref, r_ref, yl_ref, rl_ref, slope_ref, slopel_ref, u_ref, q_ref, qt_ref, k_ref, kt_ref, v_ref, vt_ref,
    p_ref, d_ref, pl_ref, dl_ref, att_ref, do_ref, dot_ref, dk_ref, dv_ref, dkl_ref, dvl_ref,
    pg_ref, pgl_ref,
):
    seq = seq_ref[0]
    col = col_ref[0]
    length = lengths_ref[col]
    base = seq * HALF
    upper = seq == 1
    active = length > base
    lanes = lax.broadcasted_iota(jnp.int32, (1, 2 * DH), 1)
    head_mask = [(lanes < DH).astype(f32).astype(bf16), (lanes >= DH).astype(f32).astype(bf16)]
    loads = [
        pltpu.make_async_copy(src, dst, sems.at[n])
        for n, (src, dst) in enumerate(((w_hbm, w_ref), (wo_hbm, wo_ref), (cot_hbm, cot_ref)))
    ]
    for load in loads:
        load.start()
    QB = HALF // 2
    parts = [slice(0, QB), slice(QB, HALF)]

    def place(half, b):
        i = 2 * half + b // 2
        return (b + col) & 1, pl.multiple_of(i * BLK, BLK)

    def features(half):
        parts = []
        for b in range(NBLK):
            src, at = place(half, b)
            part = e_ref[:, src, :, pl.ds(at, BLK)].astype(f32).reshape(D, BLK)
            parts.append(part.T)
        return jnp.concatenate(parts, axis=0)

    def put_grad(half, grad):
        flat = grad.T.reshape(D // FEAT, FEAT, HALF).astype(bf16)
        for b in range(NBLK):
            dst, at = place(half, b)
            g_ref[:, dst, :, pl.ds(at, BLK)] = flat[:, :, b * BLK : (b + 1) * BLK]

    def pairs_of(act):
        return [act[:, hp * 2 * DH : (hp + 1) * 2 * DH] for hp in range(PAIRS)]

    def project(half, blocks, yb, slopes):
        for n, blk in enumerate(blocks):
            act, slope = gate(dot_nn(yb, w_ref[:, blk * HID : (blk + 1) * HID]))
            slopes[:, n * HID : (n + 1) * HID] = slope
            act = act.astype(bf16)
            if blk == 0:
                u_ref[...] = act
            elif blk == 2:
                act = act.astype(f32) * (0.5 * DH**-0.5)
                qt_ref[...] = act.T.astype(bf16)
                for hp, part in enumerate(pairs_of(act.astype(bf16))):
                    q_ref[hp] = part
            else:
                target, turned = (v_ref, vt_ref) if blk == 1 else (k_ref, kt_ref)
                turned[half] = act.T
                for hp, part in enumerate(pairs_of(act)):
                    target[half, hp] = part

    def plus(a, b):
        return b if a is None else a + b

    def forward(hp, lower):
        q, k = q_ref[hp], k_ref[1, hp]
        if lower:
            kl = k_ref[0, hp]
        row = lax.broadcasted_iota(jnp.int32, (QB, 1), 0)
        for h in range(2):
            head = 2 * hp + h
            hs = pl.ds(pl.multiple_of(head * DH, DH), DH)
            vt = vt_ref[1, hs, :]
            qm = q * head_mask[h]
            att = [None, None]
            for qi in range(2):
                for ki in range(qi + 1):
                    half = dot_nt(qm[parts[qi]], k[parts[ki]])
                    a = 1.0 + jnp.tanh(half)
                    if ki == qi:
                        limit = jnp.minimum(row, length - 1 - base - ki * QB)
                        ok = lax.broadcasted_iota(jnp.int32, a.shape, 1) <= limit
                        a = jnp.where(ok, a, 0.0)
                    at = 2 * qi + ki
                    p = (half * a).astype(bf16)
                    p_ref[head, at] = p
                    d_ref[head, at] = a
                    att[qi] = plus(att[qi], dot_nt(vt[:, parts[ki]], p))
                if lower:
                    half = dot_nt(qm[parts[qi]], kl)
                    a = 1.0 + jnp.tanh(half)
                    p = (half * a).astype(bf16)
                    pl_ref[head, parts[qi]] = p
                    dl_ref[head, parts[qi]] = a
                    att[qi] = att[qi] + dot_nt(vt_ref[0, hs, :], p)
            att_ref[hs, :] = jnp.concatenate(att, axis=1)

    def backward(hp, lower):
        v, do = v_ref[1, hp], do_ref[hp]
        if lower:
            vl = v_ref[0, hp]
        for h in range(2):
            head = 2 * hp + h
            hs = pl.ds(pl.multiple_of(head * DH, DH), DH)
            qt = qt_ref[hs, :]
            dot = dot_ref[hs, :]
            kt = kt_ref[1, hs, :]
            dm = do * head_mask[h]
            dq = [None, None]
            dk = [None, None]
            dv = [None, None]
            if lower:
                dkl, dvl = None, None
            for qi in range(2):
                qs = parts[qi]
                for ki in range(qi + 1):
                    at = 2 * qi + ki
                    p = p_ref[head, at]
                    ds = (dot_nt(dm[qs], v[parts[ki]]) * slope_of(d_ref[head, at], p)).astype(bf16)
                    dq[qi] = plus(dq[qi], dot_nt(kt[:, parts[ki]], ds))
                    dk[ki] = plus(dk[ki], dot_nn(qt[:, qs], ds))
                    dv[ki] = plus(dv[ki], dot_nn(dot[:, qs], p))
                if lower:
                    p = pl_ref[head, qs]
                    ds = (dot_nt(dm[qs], vl) * slope_of(dl_ref[head, qs], p)).astype(bf16)
                    dq[qi] = plus(dq[qi], dot_nt(kt_ref[0, hs, :], ds))
                    dkl = plus(dkl, dot_nn(qt[:, qs], ds))
                    dvl = plus(dvl, dot_nn(dot[:, qs], p))
            att_ref[hs, :] = jnp.concatenate(dq, axis=1)
            dk_ref[hs, :] = jnp.concatenate(dk, axis=1)
            dv_ref[hs, :] = jnp.concatenate(dv, axis=1)
            if lower:
                dkl_ref[hs, :] = dkl
                dvl_ref[hs, :] = dvl

    def over_pairs(body):
        @pl.when(upper)
        def _():
            @pl.loop(0, PAIRS)
            def _(hp):
                body(hp, True)

        @pl.when(jnp.logical_not(upper))
        def _():
            @pl.loop(0, PAIRS)
            def _(hp):
                body(hp, False)

    g_ref[...] = jnp.zeros_like(g_ref)

    @pl.when(jnp.logical_not(active))
    def _():
        for load in loads:
            load.wait()
        out_ref[...] = jnp.zeros_like(out_ref)

    @pl.when(active)
    def _():
        x = features(seq)
        for load in loads:
            load.wait()
        x_ref[...] = x
        y, r = norm(x)
        y_ref[...] = y
        r_ref[...] = 0.5 * r
        project(1, (0, 1, 2, 3), (0.5 * y).astype(bf16), slope_ref)

        @pl.when(upper)
        def _():
            y, r = norm(features(0))
            yl_ref[...] = y
            rl_ref[...] = 0.5 * r
            project(0, (1, 3), (0.5 * y).astype(bf16), slopel_ref)

        over_pairs(forward)

        na, ra = norm(att_ref[...].T * (1.0 / LEN))
        u = u_ref[...].astype(f32)
        valid = (base + lax.broadcasted_iota(jnp.int32, (HALF, 1), 0)) < length
        mixed = dot_nn((na * u).astype(bf16), wo_ref[...]) + x_ref[...]
        out_ref[...] = jnp.where(valid, mixed, 0.0).astype(bf16)
        cot = jnp.where(valid, cot_ref[...].astype(f32), 0.0)
        gg = dot_nt(cot.astype(bf16), wo_ref[...])
        pg_ref[:, :HID] = (gg * na * slope_ref[:, :HID]).astype(bf16)
        da = norm_back(na, ra * (1.0 / LEN), gg * u)
        dot_ref[...] = da.T.astype(bf16)
        for hp, part in enumerate(pairs_of(da.astype(bf16))):
            do_ref[hp] = part

        over_pairs(backward)

        dq = att_ref[...].T * (0.5 * DH**-0.5)
        pg_ref[:, HID : 2 * HID] = (dv_ref[...].T * slope_ref[:, HID : 2 * HID]).astype(bf16)
        pg_ref[:, 2 * HID : 3 * HID] = (dq * slope_ref[:, 2 * HID : 3 * HID]).astype(bf16)
        pg_ref[:, 3 * HID :] = (dk_ref[...].T * slope_ref[:, 3 * HID :]).astype(bf16)
        eg = dot_nt(pg_ref[...], w_ref[...])
        cot = jnp.where(valid, cot_ref[...].astype(f32), 0.0)
        put_grad(seq, cot + norm_back(y_ref[...], r_ref[...], eg))

        @pl.when(upper)
        def _():
            pgl_ref[:, :HID] = (dvl_ref[...].T * slopel_ref[:, :HID]).astype(bf16)
            pgl_ref[:, HID:] = (dkl_ref[...].T * slopel_ref[:, HID:]).astype(bf16)
            eg = dot_nt(pgl_ref[:, :HID], w_ref[:, HID : 2 * HID])
            eg = eg + dot_nt(pgl_ref[:, HID:], w_ref[:, 3 * HID :])
            put_grad(0, norm_back(yl_ref[...], rl_ref[...], eg))


def vmem():
    return pl.BlockSpec(memory_space=pltpu.VMEM)


def hbm():
    return pl.BlockSpec(memory_space=pl.ANY)


def smem():
    return pl.BlockSpec(memory_space=pltpu.SMEM)


def in_vmem(x):
    return pltpu.with_memory_space_constraint(x, pltpu.VMEM)


def params():
    return pltpu.CompilerParams(vmem_limit_bytes=60 * 1024 * 1024)


def table_rows(table):
    return pl.pallas_call(
        rows_kernel,
        in_specs=[vmem()],
        out_specs=vmem(),
        out_shape=pltpu.VMEM((G_HI, BLK), f32),
        compiler_params=params(),
        name="table_rows",
    )(table)


def gather(seq, lengths, own, other, rows):
    return pl.pallas_call(
        gather_kernel,
        in_specs=[smem(), smem(), vmem(), vmem(), vmem()],
        out_specs=vmem(),
        out_shape=pltpu.VMEM((USERS, 2, FEAT, HALF), bf16),
        scratch_shapes=[
            pltpu.VMEM((2, NBLK, USERS, BLK), jnp.int32),
            pltpu.VMEM((2, G_STEP, BLK), jnp.int32),
            pltpu.VMEM((2, G_STEP * BLK, BLK), f32),
            pltpu.SMEM((USERS * NBLK + NBLK,), jnp.int32),
            pltpu.SMEM((2, G_STEP, BLK), jnp.int32),
            pltpu.SemaphoreType.DMA((2,)),
        ],
        compiler_params=params(),
        name="gather",
    )(seq, lengths, own, other, rows)


def scatter(seq, lengths, half, own, other, grad, dtype):
    return pl.pallas_call(
        scatter_kernel,
        in_specs=[smem(), smem(), smem(), vmem(), vmem(), vmem()],
        out_specs=vmem(),
        out_shape=pltpu.VMEM((FEAT, S_ROWS), dtype),
        scratch_shapes=[
            pltpu.VMEM((2, NBLK, USERS, BLK), jnp.int32),
            pltpu.VMEM((S_LO * FEAT, S_HI), f32),
            pltpu.SMEM((USERS * NBLK + NBLK,), jnp.int32),
        ],
        compiler_params=params(),
        name="scatter",
    )(seq, lengths, half, own, other, grad)


def layer(seq, col, lengths, e, w, wo, cot):
    return pl.pallas_call(
        layer_kernel,
        in_specs=[smem(), smem(), smem(), vmem(), hbm(), hbm(), hbm()],
        out_specs=(vmem(), vmem()),
        out_shape=(
            jax.ShapeDtypeStruct((HALF, D), bf16),
            pltpu.VMEM((USERS, 2, FEAT, HALF), bf16),
        ),
        scratch_shapes=[
            pltpu.VMEM((D, 4 * HID), bf16),
            pltpu.VMEM((HID, D), bf16),
            pltpu.VMEM((HALF, D), bf16),
            pltpu.SemaphoreType.DMA((3,)),
            pltpu.VMEM((HALF, D), f32),
            pltpu.VMEM((HALF, D), f32),
            pltpu.VMEM((HALF, 1), f32),
            pltpu.VMEM((HALF, D), f32),
            pltpu.VMEM((HALF, 1), f32),
            pltpu.VMEM((HALF, 4 * HID), f32),
            pltpu.VMEM((HALF, 2 * HID), f32),
            pltpu.VMEM((HALF, HID), bf16),
            pltpu.VMEM((PAIRS, HALF, 2 * DH), bf16),
            pltpu.VMEM((HID, HALF), bf16),
            pltpu.VMEM((2, PAIRS, HALF, 2 * DH), bf16),
            pltpu.VMEM((2, HID, HALF), bf16),
            pltpu.VMEM((2, PAIRS, HALF, 2 * DH), bf16),
            pltpu.VMEM((2, HID, HALF), bf16),
            pltpu.VMEM((H, 4, HALF // 2, HALF // 2), bf16),
            pltpu.VMEM((H, 4, HALF // 2, HALF // 2), f32),
            pltpu.VMEM((H, HALF, HALF), bf16),
            pltpu.VMEM((H, HALF, HALF), f32),
            pltpu.VMEM((HID, HALF), f32),
            pltpu.VMEM((PAIRS, HALF, 2 * DH), bf16),
            pltpu.VMEM((HID, HALF), bf16),
            pltpu.VMEM((HID, HALF), f32),
            pltpu.VMEM((HID, HALF), f32),
            pltpu.VMEM((HID, HALF), f32),
            pltpu.VMEM((HID, HALF), f32),
            pltpu.VMEM((HALF, 4 * HID), bf16),
            pltpu.VMEM((HALF, 2 * HID), bf16),
        ],
        compiler_params=params(),
        name="layer",
    )(seq, col, lengths, e, w, wo, cot)


def per_device(history_items, lengths, item_table, input_weight, output_weight, output_cotangent):
    col = lax.axis_index("col").astype(jnp.int32).reshape(1)
    seq = lax.axis_index("seq").astype(jnp.int32).reshape(1)
    swap = [(0, 1), (1, 0)]
    both = ("col", "seq")
    own = history_items
    other = in_vmem(lax.ppermute(own, "seq", swap))
    rows = in_vmem(table_rows(item_table))
    looked = gather(seq, lengths, own, other, rows)
    flat = looked.reshape(2 * USERS, FEAT, HALF)
    arrived = lax.all_to_all(flat, both, split_axis=0, concat_axis=0, tiled=True)
    arrived = in_vmem(arrived.reshape(USERS, 2, FEAT, HALF))
    out, grad = layer(
        seq, col, lengths, arrived, input_weight, output_weight, output_cotangent[0]
    )
    grad = grad.reshape(2 * USERS, FEAT, HALF)
    back = lax.all_to_all(grad, both, split_axis=0, concat_axis=0, tiled=True)
    back = in_vmem(back.reshape(USERS, 2, FEAT, HALF))
    theirs = scatter(seq, lengths, 1 - seq, own, other, back, bf16)
    received = lax.ppermute(theirs, "seq", swap)
    mine = scatter(seq, lengths, seq, own, other, back, f32)
    return (out[None], mine + received.astype(f32))


def solution(mesh):
    in_specs = (P(None, "seq"), P(), P("col", None), P(), P(), P("col", "seq", None))
    out_specs = (P("col", "seq", None), P("col", "seq"))
    return jax.shard_map(
        per_device, mesh=mesh, in_specs=in_specs, out_specs=out_specs, check_vma=False
    )
```

profile of v0, /device:TPU:1, one launch (start us, length us, event | category | flops | bytes accessed | tf_op | source)
XLA Modules:
  0.0 142.1 jit_solution(5236735515488127321)
XLA Ops:
  0.6 2.1 %collective-permute-start = (s32[64,512]{1,0:T(8,128)}, s32[64,512]{1,0:T(8,128)S(1)}, u32[]{:S(2)}, u32[]{:S(2)}) collective-permute-start(s32[64,512]{1,0:T(8,128)} %own_ref.5), channel_id=1, source_target_pairs={{0,1},{1,0},{2,3},{3,2},{4,5},{5,4},{6,7},{7,6},{8,9},{9,8},{10,11... | collective-permute-start | bytes 393224 | tf_op jit(solution)/shard_map/ppermute | solution.py:536
  2.7 2.2 %table_rows.1.rows_ref = f32[4096,128]{1,0:T(8,128)S(1)} custom-call(f32[8,65536]{1,0:T(8,128)} %table_ref.1), custom_call_target="tpu_custom_call" | custom-call | tf_op jit(solution)/shard_map/table_rows/pallas_call | solution.py:438
  4.9 0.8 collective-permute-done.other_ref
  5.7 19.7 %gather.1 = bf16[64,2,8,512]{3,2,1,0:T(8,128)(2,1)} custom-call(s32[1]{0:T(128)} %bitcast.seq_ref.half_ref, s32[64]{0:T(128)} %lengths_ref.7, s32[64,512]{1,0:T(8,128)} %own_ref.5, s32[64,512]{1,0:T(8,128)S(1)} %collective-permute-done.other_ref, f32[4096,128]{1,0:T(8,128)S(1)} %table_rows.1.rows_ref), custom_call_target="tpu_custom_call" | custom-call | tf_op jit(solution)/shard_map/gather/pallas_call | solution.py:449
  25.5 11.9 %all-to-all-start = ((bf16[128,8,512]{2,1,0:T(8,128)(2,1)}), bf16[128,8,512]{2,1,0:T(8,128)(2,1)S(1)}, u32[]{:S(2)}, u32[]{:S(2)}) async-start(bf16[128,8,512]{2,1,0:T(8,128)(2,1)} %bitcast.2), calls=%async_computation | async-start | bytes 2097152 | tf_op jit(solution)/shard_map/all_to_all | solution.py:540
  37.4 19.2 %all-to-all-done = bf16[128,8,512]{2,1,0:T(8,128)(2,1)S(1)} async-done(((bf16[128,8,512]{2,1,0:T(8,128)(2,1)}), bf16[128,8,512]{2,1,0:T(8,128)(2,1)S(1)}, u32[]{:S(2)}, u32[]{:S(2)}) %all-to-all-start) | async-done | bytes 1048608 | tf_op jit(solution)/shard_map/all_to_all | solution.py:540
  56.6 19.2 %layer.1 = (bf16[512,512]{1,0:T(8,128)(2,1)}, bf16[64,2,8,512]{3,2,1,0:T(8,128)(2,1)}) custom-call(s32[1]{0:T(128)} %bitcast.seq_ref.half_ref, s32[1]{0:T(128)} %bitcast.1.col_ref, s32[64]{0:T(128)} %lengths_ref.7, bf16[64,2,8,512]{3,2,1,0:T(8,128)(2,1)S(1)} %bitcast.10, bf16[512,2048]{1,0:T(8,128)(2,1)} %w_hbm.1, bf16[512,512]{1,0:T(8,128)(2,1)} %wo_hbm.1, ...), custom_call_target="tpu_custom_call" | custom-call | tf_op jit(solution)/shard_map/layer/pallas_call | solution.py:484
  75.8 13.4 %all-to-all-start.1 = ((bf16[128,8,512]{2,1,0:T(8,128)(2,1)}), bf16[128,8,512]{2,1,0:T(8,128)(2,1)S(1)}, u32[]{:S(2)}, u32[]{:S(2)}) async-start(bf16[128,8,512]{2,1,0:T(8,128)(2,1)} %bitcast.6), calls=%async_computation.1 | async-start | bytes 2097152 | tf_op jit(solution)/shard_map/all_to_all | solution.py:546
  89.2 19.2 %all-to-all-done.1 = bf16[128,8,512]{2,1,0:T(8,128)(2,1)S(1)} async-done(((bf16[128,8,512]{2,1,0:T(8,128)(2,1)}), bf16[128,8,512]{2,1,0:T(8,128)(2,1)S(1)}, u32[]{:S(2)}, u32[]{:S(2)}) %all-to-all-start.1) | async-done | bytes 1048608 | tf_op jit(solution)/shard_map/all_to_all | solution.py:546
  108.5 16.0 %scatter.3 = bf16[8,32768]{1,0:T(8,128)(2,1)S(1)} custom-call(s32[1]{0:T(128)} %bitcast.seq_ref.half_ref, s32[64]{0:T(128)} %lengths_ref.7, s32[1]{0:T(128)S(6)} %sub.3.half_ref, s32[64,512]{1,0:T(8,128)} %own_ref.5, s32[64,512]{1,0:T(8,128)S(1)} %collective-permute-done.other_ref, bf16[64,2,8,512]{3,2,1,0:T(8,128)(2,1)S(1)} %bitcast.8), custom_call_target="tpu_custom_call" | custom-call | tf_op jit(solution)/shard_map/scatter/pallas_call | solution.py:468
  124.5 0.4 collective-permute-start.1
  124.9 16.2 %scatter.2 = f32[8,32768]{1,0:T(8,128)S(1)} custom-call(s32[1]{0:T(128)} %bitcast.seq_ref.half_ref, s32[64]{0:T(128)} %lengths_ref.7, s32[1]{0:T(128)} %bitcast.seq_ref.half_ref, s32[64,512]{1,0:T(8,128)} %own_ref.5, s32[64,512]{1,0:T(8,128)S(1)} %collective-permute-done.other_ref, bf16[64,2,8,512]{3,2,1,0:T(8,128)(2,1)S(1)} %bitcast.9), custom_call_target="tpu_custom_call" | custom-call | tf_op jit(solution)/shard_map/scatter/pallas_call | solution.py:468
  141.0 0.0 collective-permute-done.1
  141.1 1.1 convert_add_fusion
Async XLA Ops:
  0.6 5.1 %collective-permute-start = (s32[64,512]{1,0:T(8,128)}, s32[64,512]{1,0:T(8,128)S(1)}, u32[]{:S(2)}, u32[]{:S(2)}) collective-permute-start(s32[64,512]{1,0:T(8,128)} %own_ref.5), channel_id=1, source_target_pairs={{0,1},{1,0},{2,3},{3,2},{4,5},{5,4},{6,7},{7,6},{8,9},{9,8},{10,11... | collective-permute-start | bytes 393224 | tf_op jit(solution)/shard_map/ppermute | solution.py:536
  25.5 31.1 %all-to-all-start = ((bf16[128,8,512]{2,1,0:T(8,128)(2,1)}), bf16[128,8,512]{2,1,0:T(8,128)(2,1)S(1)}, u32[]{:S(2)}, u32[]{:S(2)}) async-start(bf16[128,8,512]{2,1,0:T(8,128)(2,1)} %bitcast.2), calls=%async_computation | async-start | bytes 2097152 | tf_op jit(solution)/shard_map/all_to_all | solution.py:540
  75.8 32.6 %all-to-all-start.1 = ((bf16[128,8,512]{2,1,0:T(8,128)(2,1)}), bf16[128,8,512]{2,1,0:T(8,128)(2,1)S(1)}, u32[]{:S(2)}, u32[]{:S(2)}) async-start(bf16[128,8,512]{2,1,0:T(8,128)(2,1)} %bitcast.6), calls=%async_computation.1 | async-start | bytes 2097152 | tf_op jit(solution)/shard_map/all_to_all | solution.py:546
  124.5 16.5 %collective-permute-start.1 = (bf16[8,32768]{1,0:T(8,128)(2,1)S(1)}, bf16[8,32768]{1,0:T(8,128)(2,1)S(1)}, u32[]{:S(2)}, u32[]{:S(2)}) collective-permute-start(bf16[8,32768]{1,0:T(8,128)(2,1)S(1)} %scatter.3), channel_id=1, source_target_pairs={{0,1},{1,0},{2,3},{3,2},{4,5},{5,4},{6,7},{7,6},{8,9},{9,8},{10,11... | collective-permute-start | bytes 1572872 | tf_op jit(solution)/shard_map/ppermute | solution.py:549
where the time goes:
time: 141 us; the launch traced here: 142 us
  Pallas kernels  73.3 us (52%)
  waiting for transfers between devices  39.3 us (28%)
  starting transfers between devices  27.8 us (20%)
    pallas_call x2, Pallas kernels, scatter(): pl.pallas_call(scatter_kernel, in_specs=[smem(), smem(), smem(), vmem(),...  32.2 us
    pallas_call x1, Pallas kernels, gather(): pl.pallas_call(gather_kernel, in_specs=[smem(), smem(), vmem(), vmem(), v...  19.7 us
    all_to_all x1, waiting for transfers between devices, per_device(): back = lax.all_to_all(grad, both, split_axis=0, concat_axis=0, tiled=True)  19.2 us
    all_to_all x1, waiting for transfers between devices, per_device(): lax.all_to_all(flat, both, split_axis=0, concat_axis=0, tiled=True)  19.2 us
    pallas_call x1, Pallas kernels, layer(): pl.pallas_call(layer_kernel, in_specs=[smem(), smem(), smem(), vmem(), hb...  19.2 us
    all_to_all x1, starting transfers between devices, per_device(): back = lax.all_to_all(grad, both, split_axis=0, concat_axis=0, tiled=True)  13.4 us
    all_to_all x1, starting transfers between devices, per_device(): lax.all_to_all(flat, both, split_axis=0, concat_axis=0, tiled=True)  11.9 us
  transfers between devices with their start and end apart: 4, of which 3 were waited for; matrix products, arithmetic and copies ran while one was open for 0% of the time, Pallas kernels for 13%

commit v1 on v0

--- a/solution.py
+++ b/solution.py
@@ -17,6 +17,7 @@
 NBLK = HALF // BLK
 ROWS = 65536
 PAIRS = H // 2
+AHEAD = 2
 norm_epsilon = 1e-05
 bf16 = jnp.bfloat16
 f32 = jnp.float32
@@ -28,6 +29,7 @@
 S_LO = 32
 S_HI = S_ROWS // S_LO
 S_STEP = 16
+S_REST = 4
 
 
 def block_list(seq, lengths_ref, list_ref):
@@ -138,10 +140,10 @@
     acc_ref[...] = jnp.zeros_like(acc_ref)
     count = block_list(seq, lengths_ref, list_ref)
 
-    def step(g, carry):
+    def add(first, number):
         rows, grads = [], []
-        for j in range(S_STEP):
-            at = g * S_STEP + j
+        for j in range(number):
+            at = first + j
             b = list_ref[jnp.maximum(jnp.minimum(at, count - 1), 0)]
             row = item_row(items_ref, seq, b) - base
             rows.append(jnp.where(at < count, row, -1))
@@ -153,7 +155,7 @@
             )
         index = jnp.concatenate(rows, axis=1)
         grad = jnp.concatenate(grads, axis=1)
-        n = S_STEP * BLK
+        n = number * BLK
         lo = lax.shift_right_arithmetic(index, 10)
         hi = index & (S_HI - 1)
         mask = lax.broadcasted_iota(jnp.int32, (S_LO, FEAT, n), 0) == lo.reshape(1, 1, n)
@@ -162,9 +164,17 @@
         acc_ref[...] += lax.dot_general(
             spread, onehot(hi, S_HI), (((1,), (1,)), ((), ())), preferred_element_type=f32
         )
-        return carry
-
-    lax.fori_loop(0, (count + S_STEP - 1) // S_STEP, step, 0)
+
+    whole = lax.div(count, S_STEP)
+
+    @pl.loop(0, whole)
+    def _(g):
+        add(g * S_STEP, S_STEP)
+
+    @pl.loop(0, lax.div(count - whole * S_STEP + (S_REST - 1), S_REST))
+    def _(g):
+        add(whole * S_STEP + g * S_REST, S_REST)
+
     for lo in range(S_LO):
         out_ref[:, lo * S_HI : (lo + 1) * S_HI] = acc_ref[lo * FEAT : (lo + 1) * FEAT, :].astype(
             out_ref.dtype
@@ -270,76 +280,84 @@
     def plus(a, b):
         return b if a is None else a + b
 
+    def blocks_of(lower):
+        keys = {0: (0,), 1: (0, 1)}
+        low = (-1,) if lower else ()
+        return [(h, qi, ki) for h in range(2) for qi in range(2) for ki in keys[qi] + low]
+
+    def ahead(first, second, tasks):
+        ready = [first(*task) for task in tasks[:AHEAD]]
+        for n, task in enumerate(tasks):
+            if n + AHEAD < len(tasks):
+                ready.append(first(*tasks[n + AHEAD]))
+            second(*task, ready[n])
+
+    def rows_of(hp, h):
+        head = 2 * hp + h
+        return head, pl.ds(pl.multiple_of(head * DH, DH), DH)
+
     def forward(hp, lower):
         q, k = q_ref[hp], k_ref[1, hp]
-        if lower:
-            kl = k_ref[0, hp]
+        qm = [q * head_mask[h] for h in range(2)]
         row = lax.broadcasted_iota(jnp.int32, (QB, 1), 0)
+        att = {}
+
+        def first(h, qi, ki):
+            return dot_nt(qm[h][parts[qi]], k_ref[0, hp] if ki < 0 else k[parts[ki]])
+
+        def second(h, qi, ki, half):
+            head, hs = rows_of(hp, h)
+            a = 1.0 + jnp.tanh(half)
+            if ki == qi:
+                limit = jnp.minimum(row, length - 1 - base - ki * QB)
+                ok = lax.broadcasted_iota(jnp.int32, a.shape, 1) <= limit
+                a = jnp.where(ok, a, 0.0)
+            p = (half * a).astype(bf16)
+            if ki < 0:
+                pl_ref[head, parts[qi]] = p
+                dl_ref[head, parts[qi]] = a
+                vt = vt_ref[0, hs, :]
+            else:
+                p_ref[head, 2 * qi + ki] = p
+                d_ref[head, 2 * qi + ki] = a
+                vt = vt_ref[1, hs, parts[ki]]
+            att[h, qi] = plus(att.get((h, qi)), dot_nt(vt, p))
+
+        ahead(first, second, blocks_of(lower))
         for h in range(2):
-            head = 2 * hp + h
-            hs = pl.ds(pl.multiple_of(head * DH, DH), DH)
-            vt = vt_ref[1, hs, :]
-            qm = q * head_mask[h]
-            att = [None, None]
-            for qi in range(2):
-                for ki in range(qi + 1):
-                    half = dot_nt(qm[parts[qi]], k[parts[ki]])
-                    a = 1.0 + jnp.tanh(half)
-                    if ki == qi:
-                        limit = jnp.minimum(row, length - 1 - base - ki * QB)
-                        ok = lax.broadcasted_iota(jnp.int32, a.shape, 1) <= limit
-                        a = jnp.where(ok, a, 0.0)
-                    at = 2 * qi + ki
-                    p = (half * a).astype(bf16)
-                    p_ref[head, at] = p
-                    d_ref[head, at] = a
-                    att[qi] = plus(att[qi], dot_nt(vt[:, parts[ki]], p))
-                if lower:
-                    half = dot_nt(qm[parts[qi]], kl)
-                    a = 1.0 + jnp.tanh(half)
-                    p = (half * a).astype(bf16)
-                    pl_ref[head, parts[qi]] = p
-                    dl_ref[head, parts[qi]] = a
-                    att[qi] = att[qi] + dot_nt(vt_ref[0, hs, :], p)
-            att_ref[hs, :] = jnp.concatenate(att, axis=1)
+            att_ref[rows_of(hp, h)[1], :] = jnp.concatenate([att[h, 0], att[h, 1]], axis=1)
 
     def backward(hp, lower):
         v, do = v_ref[1, hp], do_ref[hp]
-        if lower:
-            vl = v_ref[0, hp]
+        dm = [do * head_mask[h] for h in range(2)]
+        dq, dk, dv = {}, {}, {}
+
+        def first(h, qi, ki):
+            return dot_nt(dm[h][parts[qi]], v_ref[0, hp] if ki < 0 else v[parts[ki]])
+
+        def second(h, qi, ki, dp):
+            head, hs = rows_of(hp, h)
+            qs = parts[qi]
+            if ki < 0:
+                p, a = pl_ref[head, qs], dl_ref[head, qs]
+                kt = kt_ref[0, hs, :]
+            else:
+                p, a = p_ref[head, 2 * qi + ki], d_ref[head, 2 * qi + ki]
+                kt = kt_ref[1, hs, parts[ki]]
+            ds = (dp * slope_of(a, p)).astype(bf16)
+            dq[h, qi] = plus(dq.get((h, qi)), dot_nt(kt, ds))
+            dk[h, ki] = plus(dk.get((h, ki)), dot_nn(qt_ref[hs, qs], ds))
+            dv[h, ki] = plus(dv.get((h, ki)), dot_nn(dot_ref[hs, qs], p))
+
+        ahead(first, second, blocks_of(lower))
         for h in range(2):
-            head = 2 * hp + h
-            hs = pl.ds(pl.multiple_of(head * DH, DH), DH)
-            qt = qt_ref[hs, :]
-            dot = dot_ref[hs, :]
-            kt = kt_ref[1, hs, :]
-            dm = do * head_mask[h]
-            dq = [None, None]
-            dk = [None, None]
-            dv = [None, None]
+            hs = rows_of(hp, h)[1]
+            att_ref[hs, :] = jnp.concatenate([dq[h, 0], dq[h, 1]], axis=1)
+            dk_ref[hs, :] = jnp.concatenate([dk[h, 0], dk[h, 1]], axis=1)
+            dv_ref[hs, :] = jnp.concatenate([dv[h, 0], dv[h, 1]], axis=1)
             if lower:
-                dkl, dvl = None, None
-            for qi in range(2):
-                qs = parts[qi]
-                for ki in range(qi + 1):
-                    at = 2 * qi + ki
-                    p = p_ref[head, at]
-                    ds = (dot_nt(dm[qs], v[parts[ki]]) * slope_of(d_ref[head, at], p)).astype(bf16)
-                    dq[qi] = plus(dq[qi], dot_nt(kt[:, parts[ki]], ds))
-                    dk[ki] = plus(dk[ki], dot_nn(qt[:, qs], ds))
-                    dv[ki] = plus(dv[ki], dot_nn(dot[:, qs], p))
-                if lower:
-                    p = pl_ref[head, qs]
-                    ds = (dot_nt(dm[qs], vl) * slope_of(dl_ref[head, qs], p)).astype(bf16)
-                    dq[qi] = plus(dq[qi], dot_nt(kt_ref[0, hs, :], ds))
-                    dkl = plus(dkl, dot_nn(qt[:, qs], ds))
-                    dvl = plus(dvl, dot_nn(dot[:, qs], p))
-            att_ref[hs, :] = jnp.concatenate(dq, axis=1)
-            dk_ref[hs, :] = jnp.concatenate(dk, axis=1)
-            dv_ref[hs, :] = jnp.concatenate(dv, axis=1)
-            if lower:
-                dkl_ref[hs, :] = dkl
-                dvl_ref[hs, :] = dvl
+                dkl_ref[hs, :] = dk[h, -1]
+                dvl_ref[hs, :] = dv[h, -1]
 
     def over_pairs(body):
         @pl.when(upper)

time: 141 us -> 137 us (0.972)
  Pallas kernels: 73.3 us -> 70.3 us
  starting transfers between devices: 27.8 us -> 25.7 us
    pallas_call x1, Pallas kernels: 19.2 us -> 16.8 us  [layer(): pl.pallas_call(layer_kernel, in_specs=[smem(), smem(), smem(), vmem(), hb...]
    all_to_all x1, starting transfers between devices: 13.4 us -> 11.6 us  [per_device(): back = lax.all_to_all(grad, both, split_axis=0, concat_axis=0, tiled=True)]
where the time goes in v1:
time: 137 us
  Pallas kernels  70.3 us (51%)
  waiting for transfers between devices  39.3 us (29%)
  starting transfers between devices  25.7 us (19%)
    pallas_call x2, Pallas kernels, scatter(): pl.pallas_call(scatter_kernel, in_specs=[smem(), smem(), smem(), vmem(),...  31.6 us
    pallas_call x1, Pallas kernels, gather(): pl.pallas_call(gather_kernel, in_specs=[smem(), smem(), vmem(), vmem(), v...  19.7 us
    all_to_all x1, waiting for transfers between devices, per_device(): back = lax.all_to_all(grad, both, split_axis=0, concat_axis=0, tiled=True)  19.2 us
    all_to_all x1, waiting for transfers between devices, per_device(): lax.all_to_all(flat, both, split_axis=0, concat_axis=0, tiled=True)  19.2 us
    pallas_call x1, Pallas kernels, layer(): pl.pallas_call(layer_kernel, in_specs=[smem(), smem(), smem(), vmem(), hb...  16.8 us
    all_to_all x1, starting transfers between devices, per_device(): lax.all_to_all(flat, both, split_axis=0, concat_axis=0, tiled=True)  11.9 us
    all_to_all x1, starting transfers between devices, per_device(): back = lax.all_to_all(grad, both, split_axis=0, concat_axis=0, tiled=True)  11.6 us
  transfers between devices with their start and end apart: 4, of which 3 were waited for; matrix products, arithmetic and copies ran while one was open for 0% of the time, Pallas kernels for 13%

profile of v1, /device:TPU:1, one launch (start us, length us, event | category | flops | bytes accessed | tf_op | source)
XLA Modules:
  0.0 137.0 jit_solution(15774313670418456075)
XLA Ops:
  0.6 2.1 %collective-permute-start = (s32[64,512]{1,0:T(8,128)}, s32[64,512]{1,0:T(8,128)S(1)}, u32[]{:S(2)}, u32[]{:S(2)}) collective-permute-start(s32[64,512]{1,0:T(8,128)} %own_ref.5), channel_id=1, source_target_pairs={{0,1},{1,0},{2,3},{3,2},{4,5},{5,4},{6,7},{7,6},{8,9},{9,8},{10,11... | collective-permute-start | bytes 393224 | tf_op jit(solution)/shard_map/ppermute | solution.py:554
  2.7 2.2 %table_rows.1.rows_ref = f32[4096,128]{1,0:T(8,128)S(1)} custom-call(f32[8,65536]{1,0:T(8,128)} %table_ref.1), custom_call_target="tpu_custom_call" | custom-call | tf_op jit(solution)/shard_map/table_rows/pallas_call | solution.py:456
  4.9 0.8 collective-permute-done.other_ref
  5.7 19.7 %gather.1 = bf16[64,2,8,512]{3,2,1,0:T(8,128)(2,1)} custom-call(s32[1]{0:T(128)} %bitcast.seq_ref.half_ref, s32[64]{0:T(128)} %lengths_ref.7, s32[64,512]{1,0:T(8,128)} %own_ref.5, s32[64,512]{1,0:T(8,128)S(1)} %collective-permute-done.other_ref, f32[4096,128]{1,0:T(8,128)S(1)} %table_rows.1.rows_ref), custom_call_target="tpu_custom_call" | custom-call | tf_op jit(solution)/shard_map/gather/pallas_call | solution.py:467
  25.5 11.9 %all-to-all-start = ((bf16[128,8,512]{2,1,0:T(8,128)(2,1)}), bf16[128,8,512]{2,1,0:T(8,128)(2,1)S(1)}, u32[]{:S(2)}, u32[]{:S(2)}) async-start(bf16[128,8,512]{2,1,0:T(8,128)(2,1)} %bitcast.2), calls=%async_computation | async-start | bytes 2097152 | tf_op jit(solution)/shard_map/all_to_all | solution.py:558
  37.4 19.2 %all-to-all-done = bf16[128,8,512]{2,1,0:T(8,128)(2,1)S(1)} async-done(((bf16[128,8,512]{2,1,0:T(8,128)(2,1)}), bf16[128,8,512]{2,1,0:T(8,128)(2,1)S(1)}, u32[]{:S(2)}, u32[]{:S(2)}) %all-to-all-start) | async-done | bytes 1048608 | tf_op jit(solution)/shard_map/all_to_all | solution.py:558
  56.6 16.8 %layer.1 = (bf16[512,512]{1,0:T(8,128)(2,1)}, bf16[64,2,8,512]{3,2,1,0:T(8,128)(2,1)}) custom-call(s32[1]{0:T(128)} %bitcast.seq_ref.half_ref, s32[1]{0:T(128)} %bitcast.1.col_ref, s32[64]{0:T(128)} %lengths_ref.7, bf16[64,2,8,512]{3,2,1,0:T(8,128)(2,1)S(1)} %bitcast.10, bf16[512,2048]{1,0:T(8,128)(2,1)} %w_hbm.1, bf16[512,512]{1,0:T(8,128)(2,1)} %wo_hbm.1, ...), custom_call_target="tpu_custom_call" | custom-call | tf_op jit(solution)/shard_map/layer/pallas_call | solution.py:502
  73.4 11.6 %all-to-all-start.1 = ((bf16[128,8,512]{2,1,0:T(8,128)(2,1)}), bf16[128,8,512]{2,1,0:T(8,128)(2,1)S(1)}, u32[]{:S(2)}, u32[]{:S(2)}) async-start(bf16[128,8,512]{2,1,0:T(8,128)(2,1)} %bitcast.6), calls=%async_computation.1 | async-start | bytes 2097152 | tf_op jit(solution)/shard_map/all_to_all | solution.py:564
  85.0 19.2 %all-to-all-done.1 = bf16[128,8,512]{2,1,0:T(8,128)(2,1)S(1)} async-done(((bf16[128,8,512]{2,1,0:T(8,128)(2,1)}), bf16[128,8,512]{2,1,0:T(8,128)(2,1)S(1)}, u32[]{:S(2)}, u32[]{:S(2)}) %all-to-all-start.1) | async-done | bytes 1048608 | tf_op jit(solution)/shard_map/all_to_all | solution.py:564
  104.2 15.8 %scatter.3 = bf16[8,32768]{1,0:T(8,128)(2,1)S(1)} custom-call(s32[1]{0:T(128)} %bitcast.seq_ref.half_ref, s32[64]{0:T(128)} %lengths_ref.7, s32[1]{0:T(128)S(6)} %sub.3.half_ref, s32[64,512]{1,0:T(8,128)} %own_ref.5, s32[64,512]{1,0:T(8,128)S(1)} %collective-permute-done.other_ref, bf16[64,2,8,512]{3,2,1,0:T(8,128)(2,1)S(1)} %bitcast.8), custom_call_target="tpu_custom_call" | custom-call | tf_op jit(solution)/shard_map/scatter/pallas_call | solution.py:486
  120.0 0.1 collective-permute-start.1
  120.1 15.8 %scatter.2 = f32[8,32768]{1,0:T(8,128)S(1)} custom-call(s32[1]{0:T(128)} %bitcast.seq_ref.half_ref, s32[64]{0:T(128)} %lengths_ref.7, s32[1]{0:T(128)} %bitcast.seq_ref.half_ref, s32[64,512]{1,0:T(8,128)} %own_ref.5, s32[64,512]{1,0:T(8,128)S(1)} %collective-permute-done.other_ref, bf16[64,2,8,512]{3,2,1,0:T(8,128)(2,1)S(1)} %bitcast.9), custom_call_target="tpu_custom_call" | custom-call | tf_op jit(solution)/shard_map/scatter/pallas_call | solution.py:486
  135.9 0.0 collective-permute-done.1
  135.9 1.1 convert_add_fusion
Async XLA Ops:
  0.6 5.1 %collective-permute-start = (s32[64,512]{1,0:T(8,128)}, s32[64,512]{1,0:T(8,128)S(1)}, u32[]{:S(2)}, u32[]{:S(2)}) collective-permute-start(s32[64,512]{1,0:T(8,128)} %own_ref.5), channel_id=1, source_target_pairs={{0,1},{1,0},{2,3},{3,2},{4,5},{5,4},{6,7},{7,6},{8,9},{9,8},{10,11... | collective-permute-start | bytes 393224 | tf_op jit(solution)/shard_map/ppermute | solution.py:554
  25.5 31.1 %all-to-all-start = ((bf16[128,8,512]{2,1,0:T(8,128)(2,1)}), bf16[128,8,512]{2,1,0:T(8,128)(2,1)S(1)}, u32[]{:S(2)}, u32[]{:S(2)}) async-start(bf16[128,8,512]{2,1,0:T(8,128)(2,1)} %bitcast.2), calls=%async_computation | async-start | bytes 2097152 | tf_op jit(solution)/shard_map/all_to_all | solution.py:558
  73.4 30.8 %all-to-all-start.1 = ((bf16[128,8,512]{2,1,0:T(8,128)(2,1)}), bf16[128,8,512]{2,1,0:T(8,128)(2,1)S(1)}, u32[]{:S(2)}, u32[]{:S(2)}) async-start(bf16[128,8,512]{2,1,0:T(8,128)(2,1)} %bitcast.6), calls=%async_computation.1 | async-start | bytes 2097152 | tf_op jit(solution)/shard_map/all_to_all | solution.py:564
  120.0 15.9 %collective-permute-start.1 = (bf16[8,32768]{1,0:T(8,128)(2,1)S(1)}, bf16[8,32768]{1,0:T(8,128)(2,1)S(1)}, u32[]{:S(2)}, u32[]{:S(2)}) collective-permute-start(bf16[8,32768]{1,0:T(8,128)(2,1)S(1)} %scatter.3), channel_id=1, source_target_pairs={{0,1},{1,0},{2,3},{3,2},{4,5},{5,4},{6,7},{7,6},{8,9},{9,8},{10,11... | collective-permute-start | bytes 1572872 | tf_op jit(solution)/shard_map/ppermute | solution.py:567
